TPU v7x, 256 devices: a whole 4x4x8 slice. The times are simulated.
256 devices in a mesh: chain: 8 (over x, core), col: 32 (over y, z).
Axes of the slice: x: 4, y: 4, z: 8, core: 2. Of those that a mesh axis runs over, the one named last changes fastest.
Arguments:
- rhs: float32 [8, 32, 64, 128], P('chain', 'col'), may hold values from -6 to 6
- inverse: float32 [8, 32, 128, 128], P('chain', 'col'), as said below
- factor: float32 [8, 32, 8, 128, 128], P('chain', 'col'), may hold values from -0.1875 to 0.1875
- pattern: int32 [8, 32, 8], P('chain', 'col'), may hold values from 0 to 31, as said below
Outputs:
- forward: float32 [8, 32, 64, 128], P('chain', 'col')
- solution: float32 [8, 32, 64, 128], P('chain', 'col')
Inputs may be any that keep to these rules, and one draw needn't show every extreme that they name: `pattern`: the 8 block rows of one supernode are distinct. `inverse`: each block is lower triangular, its diagonal between 0.5 and 1.5.
All inputs are finite; a program needn't handle non-finite values.
Results may differ from a plain program's by a relative error of at most 0.00012.
Values sent between devices are 32-bit elements; how exact they have to be, the bound alone decides.
No kernel may reach another device: no remote copies, remote signals or barrier semaphores. Data moves between devices by JAX's collectives and lax.ppermute only.
A program may use at most 64 MiB of HBM per device.

v0:
```python
import jax
import jax.numpy as jnp
from jax import lax
from jax.sharding import PartitionSpec as P


def shifted(value, axis, steps):
    count = lax.axis_size(axis)
    first, last = (max(0, -steps), min(count, count - steps))
    return lax.ppermute(value, axis, [(source, source + steps) for source in range(first, last)])


def body(rhs, inverse, factor, pattern):
    levels = lax.axis_size("chain")
    supers = lax.axis_size("col")
    highest = lax.Precision.HIGHEST
    loads_block = rhs[0, 0]
    diag_inverse = inverse[0, 0]
    blocks = factor[0, 0]
    targets = pattern[0, 0]
    loads, width = loads_block.shape
    place = lax.axis_index("chain")
    onehot = (targets[:, None] == jnp.arange(supers, dtype=jnp.int32)[None, :]).astype(jnp.float32)
    pieces = 1
    rows = loads // pieces
    steps = levels + pieces - 1

    def window(step, lag):
        index = step - lag
        live = (index >= 0) & (index < pieces)
        start = jnp.clip(index, 0, pieces - 1) * rows
        return (live, start)

    def forward_step(step, carry):
        solved, incoming = carry
        live, start = window(step, place)
        residue = loads_block - incoming
        fresh = jnp.dot(residue, diag_inverse.T, precision=highest)
        solved = jnp.where(live, fresh, solved)
        terms = jnp.einsum("rb,kab->kra", fresh, blocks, precision=highest)
        summed_rows = lax.psum_scatter(
            jnp.einsum("kc,kra->cra", onehot, terms, precision=highest),
            "col",
            scatter_dimension=0,
            tiled=True,
        )[0]
        arrived = shifted(summed_rows, "chain", 1)
        got, into = window(step + 1, place)
        got = got & (place > 0)
        incoming = jnp.where(got, arrived, incoming)
        return (solved, incoming)

    empty = jnp.zeros((loads, width), jnp.float32)
    solved, unused = lax.fori_loop(0, steps, forward_step, (empty, empty))

    def backward_step(step, carry):
        answer, outgoing = carry
        lag = levels - 1 - place
        live, start = window(step, lag)
        residue = solved - outgoing
        fresh = jnp.dot(residue, diag_inverse, precision=highest)
        answer = jnp.where(live, fresh, answer)
        arrived = shifted(fresh, "chain", -1)
        picked = jnp.einsum(
            "kc,cra->kra",
            onehot,
            lax.all_gather(arrived[None], "col", axis=0, tiled=True),
            precision=highest,
        )
        term = jnp.einsum("kra,kab->rb", picked, blocks, precision=highest)
        got, into = window(step, lag - 1)
        got = got & (place < levels - 1)
        outgoing = jnp.where(got, term, outgoing)
        return (answer, outgoing)

    answer, unused_rows = lax.fori_loop(0, steps, backward_step, (empty, empty))
    return (solved[None, None], answer[None, None])


def solution(mesh):
    in_specs = (
        P("chain", "col", None, None),
        P("chain", "col", None, None),
        P("chain", "col", None, None, None),
        P("chain", "col", None),
    )
    out_specs = (P("chain", "col", None, None), P("chain", "col", None, None))
    return jax.shard_map(body, mesh=mesh, in_specs=in_specs, out_specs=out_specs, check_vma=False)
```

profile of v0, /device:TPU:2, one launch (start us, length us, event | category | flops | bytes accessed | tf_op | source)
XLA Modules:
  0.0 2476.0 jit_solution(1854762112092310647)
XLA Ops:
  7.8 1795.3 %while.35 = (s32[]{:T(128)}, f32[64,128]{1,0:T(8,128)S(1)}, f32[64,128]{1,0:T(8,128)S(1)}, s32[]{:T(128)}, f32[64,128]{1,0:T(8,128)}, /*index=5*/f32[128,128]{1,...) while((s32[]{:T(128)}, f32[64,128]{1,0:T(8,128)S(1)}, ...), condition=%wide.region_2.3_spmd.clone, body=%wide.region_0.2_spmd.clone.sunk | while | flops 138461696 | bytes 7930159 | solution.py:54
  9.0 1.7 fusion.53
  11.8 1.6 copy.25
  13.4 217.5 %reduce-scatter.2.cloned.1.call-done = f32[1,64,128]{2,1,0:T(8,128)} async-done(((f32[32,64,128]{2,1,0:T(8,128)}), f32[1,64,128]{2,1,0:T(8,128)}) %reduce-scatter.2.cloned.1.call-update) | async-done | bytes 32784 | tf_op jit(solution)/shard_map/while/body/eval_jaxpr/reduce_scatter | solution.py:41
  230.8 1.9 collective-permute-start
  232.8 3.5 collective-permute-done
  237.5 1.7 fusion.53
  240.3 1.6 copy.25
  241.9 212.8 %reduce-scatter.2.cloned.1.call-done = f32[1,64,128]{2,1,0:T(8,128)} async-done(((f32[32,64,128]{2,1,0:T(8,128)}), f32[1,64,128]{2,1,0:T(8,128)}) %reduce-scatter.2.cloned.1.call-update) | async-done | bytes 32784 | tf_op jit(solution)/shard_map/while/body/eval_jaxpr/reduce_scatter | solution.py:41
  454.7 1.9 collective-permute-start
  456.6 3.5 collective-permute-done
  461.3 1.7 fusion.53
  464.1 1.6 copy.25
  465.7 212.8 %reduce-scatter.2.cloned.1.call-done = f32[1,64,128]{2,1,0:T(8,128)} async-done(((f32[32,64,128]{2,1,0:T(8,128)}), f32[1,64,128]{2,1,0:T(8,128)}) %reduce-scatter.2.cloned.1.call-update) | async-done | bytes 32784 | tf_op jit(solution)/shard_map/while/body/eval_jaxpr/reduce_scatter | solution.py:41
  678.5 1.9 collective-permute-start
  680.4 3.5 collective-permute-done
  685.1 1.7 fusion.53
  687.9 1.6 copy.25
  689.5 212.8 %reduce-scatter.2.cloned.1.call-done = f32[1,64,128]{2,1,0:T(8,128)} async-done(((f32[32,64,128]{2,1,0:T(8,128)}), f32[1,64,128]{2,1,0:T(8,128)}) %reduce-scatter.2.cloned.1.call-update) | async-done | bytes 32784 | tf_op jit(solution)/shard_map/while/body/eval_jaxpr/reduce_scatter | solution.py:41
  902.3 1.9 collective-permute-start
  904.2 3.5 collective-permute-done
  908.9 1.7 fusion.53
  911.7 1.6 copy.25
  913.3 212.8 %reduce-scatter.2.cloned.1.call-done = f32[1,64,128]{2,1,0:T(8,128)} async-done(((f32[32,64,128]{2,1,0:T(8,128)}), f32[1,64,128]{2,1,0:T(8,128)}) %reduce-scatter.2.cloned.1.call-update) | async-done | bytes 32784 | tf_op jit(solution)/shard_map/while/body/eval_jaxpr/reduce_scatter | solution.py:41
  1126.2 1.9 collective-permute-start
  1128.1 3.5 collective-permute-done
  1132.8 1.7 fusion.53
  1135.6 1.6 copy.25
  1137.2 212.9 %reduce-scatter.2.cloned.1.call-done = f32[1,64,128]{2,1,0:T(8,128)} async-done(((f32[32,64,128]{2,1,0:T(8,128)}), f32[1,64,128]{2,1,0:T(8,128)}) %reduce-scatter.2.cloned.1.call-update) | async-done | bytes 32784 | tf_op jit(solution)/shard_map/while/body/eval_jaxpr/reduce_scatter | solution.py:41
  1350.1 1.9 collective-permute-start
  1352.0 3.5 collective-permute-done
  1356.7 1.7 fusion.53
  1361.1 212.8 %reduce-scatter.2.cloned.1.call-done = f32[1,64,128]{2,1,0:T(8,128)} async-done(((f32[32,64,128]{2,1,0:T(8,128)}), f32[1,64,128]{2,1,0:T(8,128)}) %reduce-scatter.2.cloned.1.call-update) | async-done | bytes 32784 | tf_op jit(solution)/shard_map/while/body/eval_jaxpr/reduce_scatter | solution.py:41
  1573.9 1.9 collective-permute-start
  1575.8 3.5 collective-permute-done
  1580.5 1.7 fusion.53
  1584.9 212.7 %reduce-scatter.2.cloned.1.call-done = f32[1,64,128]{2,1,0:T(8,128)} async-done(((f32[32,64,128]{2,1,0:T(8,128)}), f32[1,64,128]{2,1,0:T(8,128)}) %reduce-scatter.2.cloned.1.call-update) | async-done | bytes 32784 | tf_op jit(solution)/shard_map/while/body/eval_jaxpr/reduce_scatter | solution.py:41
  1797.7 1.9 collective-permute-start
  1799.6 3.5 collective-permute-done
  1803.1 665.7 %while.36 = (s32[]{:T(128)}, f32[64,128]{1,0:T(8,128)S(1)}, f32[64,128]{1,0:T(8,128)S(1)}, s32[]{:T(128)}, f32[64,128]{1,0:T(8,128)S(1)}, /*index=5*/f32[128,128...) while((s32[]{:T(128)}, f32[64,128]{1,0:T(8,128)S(1)}, ...), condition=%wide.region_4.5_spmd.clone, body=%wide.region_3.4_spmd.clone.sunk | while | flops 138461696 | bytes 7995759 | solution.py:76
  1804.2 1.9 collective-permute-start.1
  1808.4 75.5 %all-gather.6.cloned.1.call-done = f32[2048,128]{1,0:T(8,128)} async-done(((f32[64,128]{1,0:T(8,128)}), f32[2048,128]{1,0:T(8,128)}) %all-gather.6.cloned.1.call-update) | async-done | bytes 1048592 | tf_op jit(solution)/shard_map/while/body/eval_jaxpr/all_gather | solution.py:67
  1883.9 2.5 fusion.59
  1888.0 1.9 collective-permute-start.1
  1892.2 74.9 %all-gather.6.cloned.1.call-done = f32[2048,128]{1,0:T(8,128)} async-done(((f32[64,128]{1,0:T(8,128)}), f32[2048,128]{1,0:T(8,128)}) %all-gather.6.cloned.1.call-update) | async-done | bytes 1048592 | tf_op jit(solution)/shard_map/while/body/eval_jaxpr/all_gather | solution.py:67
  1967.0 2.5 fusion.59
  1971.1 1.9 collective-permute-start.1
  1975.3 74.9 %all-gather.6.cloned.1.call-done = f32[2048,128]{1,0:T(8,128)} async-done(((f32[64,128]{1,0:T(8,128)}), f32[2048,128]{1,0:T(8,128)}) %all-gather.6.cloned.1.call-update) | async-done | bytes 1048592 | tf_op jit(solution)/shard_map/while/body/eval_jaxpr/all_gather | solution.py:67
  2050.2 2.5 fusion.59
  2054.3 1.9 collective-permute-start.1
  2058.4 74.9 %all-gather.6.cloned.1.call-done = f32[2048,128]{1,0:T(8,128)} async-done(((f32[64,128]{1,0:T(8,128)}), f32[2048,128]{1,0:T(8,128)}) %all-gather.6.cloned.1.call-update) | async-done | bytes 1048592 | tf_op jit(solution)/shard_map/while/body/eval_jaxpr/all_gather | solution.py:67
  2133.3 2.5 fusion.59
  2137.4 1.9 collective-permute-start.1
  2141.5 74.9 %all-gather.6.cloned.1.call-done = f32[2048,128]{1,0:T(8,128)} async-done(((f32[64,128]{1,0:T(8,128)}), f32[2048,128]{1,0:T(8,128)}) %all-gather.6.cloned.1.call-update) | async-done | bytes 1048592 | tf_op jit(solution)/shard_map/while/body/eval_jaxpr/all_gather | solution.py:67
  2216.4 2.5 fusion.59
  2220.5 1.9 collective-permute-start.1
  2224.7 74.9 %all-gather.6.cloned.1.call-done = f32[2048,128]{1,0:T(8,128)} async-done(((f32[64,128]{1,0:T(8,128)}), f32[2048,128]{1,0:T(8,128)}) %all-gather.6.cloned.1.call-update) | async-done | bytes 1048592 | tf_op jit(solution)/shard_map/while/body/eval_jaxpr/all_gather | solution.py:67
  2299.6 2.5 fusion.59
  2303.7 1.9 collective-permute-start.1
  2307.8 74.9 %all-gather.6.cloned.1.call-done = f32[2048,128]{1,0:T(8,128)} async-done(((f32[64,128]{1,0:T(8,128)}), f32[2048,128]{1,0:T(8,128)}) %all-gather.6.cloned.1.call-update) | async-done | bytes 1048592 | tf_op jit(solution)/shard_map/while/body/eval_jaxpr/all_gather | solution.py:67
  2382.7 2.5 fusion.59
  2386.8 1.9 collective-permute-start.1
  2390.9 74.9 %all-gather.6.cloned.1.call-done = f32[2048,128]{1,0:T(8,128)} async-done(((f32[64,128]{1,0:T(8,128)}), f32[2048,128]{1,0:T(8,128)}) %all-gather.6.cloned.1.call-update) | async-done | bytes 1048592 | tf_op jit(solution)/shard_map/while/body/eval_jaxpr/all_gather | solution.py:67
  2465.8 2.5 fusion.59
  (124 shorter events, 52.5 us)
Async XLA Ops:
  7.2 0.7 copy-start.4
  7.8 223.0 %reduce-scatter.2.cloned.1.call-start = ((), (), s32[]{:S(2)}) async-start(), calls=%async_computation.1 | async-start | bytes 1081344 | tf_op jit(solution)/shard_map/while/body/eval_jaxpr/reduce_scatter | solution.py:41
  230.8 5.4 collective-permute-start
  236.3 218.4 %reduce-scatter.2.cloned.1.call-start = ((), (), s32[]{:S(2)}) async-start(), calls=%async_computation.1 | async-start | bytes 1081344 | tf_op jit(solution)/shard_map/while/body/eval_jaxpr/reduce_scatter | solution.py:41
  454.7 5.4 collective-permute-start
  460.1 218.4 %reduce-scatter.2.cloned.1.call-start = ((), (), s32[]{:S(2)}) async-start(), calls=%async_computation.1 | async-start | bytes 1081344 | tf_op jit(solution)/shard_map/while/body/eval_jaxpr/reduce_scatter | solution.py:41
  678.5 5.4 collective-permute-start
  683.9 218.3 %reduce-scatter.2.cloned.1.call-start = ((), (), s32[]{:S(2)}) async-start(), calls=%async_computation.1 | async-start | bytes 1081344 | tf_op jit(solution)/shard_map/while/body/eval_jaxpr/reduce_scatter | solution.py:41
  902.3 5.4 collective-permute-start
  907.7 218.4 %reduce-scatter.2.cloned.1.call-start = ((), (), s32[]{:S(2)}) async-start(), calls=%async_computation.1 | async-start | bytes 1081344 | tf_op jit(solution)/shard_map/while/body/eval_jaxpr/reduce_scatter | solution.py:41
  1126.2 5.4 collective-permute-start
  1131.6 218.5 %reduce-scatter.2.cloned.1.call-start = ((), (), s32[]{:S(2)}) async-start(), calls=%async_computation.1 | async-start | bytes 1081344 | tf_op jit(solution)/shard_map/while/body/eval_jaxpr/reduce_scatter | solution.py:41
  1350.1 5.4 collective-permute-start
  1355.5 218.4 %reduce-scatter.2.cloned.1.call-start = ((), (), s32[]{:S(2)}) async-start(), calls=%async_computation.1 | async-start | bytes 1081344 | tf_op jit(solution)/shard_map/while/body/eval_jaxpr/reduce_scatter | solution.py:41
  1573.9 5.4 collective-permute-start
  1579.3 218.3 %reduce-scatter.2.cloned.1.call-start = ((), (), s32[]{:S(2)}) async-start(), calls=%async_computation.1 | async-start | bytes 1081344 | tf_op jit(solution)/shard_map/while/body/eval_jaxpr/reduce_scatter | solution.py:41
  1797.7 5.4 collective-permute-start
  1803.1 80.8 %all-gather.6.cloned.1.call-start = ((), (), s32[]{:S(2)}) async-start(), calls=%async_computation.2 | async-start | bytes 1081344 | tf_op jit(solution)/shard_map/while/body/eval_jaxpr/all_gather | solution.py:67
  1804.2 3.5 collective-permute-start.1
  1807.7 0.6 copy-start.3
  1883.9 2.5 copy-start
  1886.9 80.1 %all-gather.6.cloned.1.call-start = ((), (), s32[]{:S(2)}) async-start(), calls=%async_computation.2 | async-start | bytes 1081344 | tf_op jit(solution)/shard_map/while/body/eval_jaxpr/all_gather | solution.py:67
  1888.0 3.5 collective-permute-start.1
  1891.5 0.6 copy-start.3
  1967.0 2.5 copy-start
  1970.0 80.1 %all-gather.6.cloned.1.call-start = ((), (), s32[]{:S(2)}) async-start(), calls=%async_computation.2 | async-start | bytes 1081344 | tf_op jit(solution)/shard_map/while/body/eval_jaxpr/all_gather | solution.py:67
  1971.1 3.5 collective-permute-start.1
  1974.6 0.6 copy-start.3
  2050.2 2.5 copy-start
  2053.2 80.1 %all-gather.6.cloned.1.call-start = ((), (), s32[]{:S(2)}) async-start(), calls=%async_computation.2 | async-start | bytes 1081344 | tf_op jit(solution)/shard_map/while/body/eval_jaxpr/all_gather | solution.py:67
  2054.3 3.5 collective-permute-start.1
  2057.8 0.6 copy-start.3
  2133.3 2.5 copy-start
  2136.3 80.1 %all-gather.6.cloned.1.call-start = ((), (), s32[]{:S(2)}) async-start(), calls=%async_computation.2 | async-start | bytes 1081344 | tf_op jit(solution)/shard_map/while/body/eval_jaxpr/all_gather | solution.py:67
  2137.4 3.5 collective-permute-start.1
  2140.9 0.6 copy-start.3
  2216.4 2.5 copy-start
  2219.4 80.1 %all-gather.6.cloned.1.call-start = ((), (), s32[]{:S(2)}) async-start(), calls=%async_computation.2 | async-start | bytes 1081344 | tf_op jit(solution)/shard_map/while/body/eval_jaxpr/all_gather | solution.py:67
  2220.5 3.5 collective-permute-start.1
  2224.0 0.6 copy-start.3
  2299.6 2.5 copy-start
  2302.6 80.1 %all-gather.6.cloned.1.call-start = ((), (), s32[]{:S(2)}) async-start(), calls=%async_computation.2 | async-start | bytes 1081344 | tf_op jit(solution)/shard_map/while/body/eval_jaxpr/all_gather | solution.py:67
  2303.7 3.5 collective-permute-start.1
  2307.2 0.6 copy-start.3
  2382.7 2.5 copy-start
  2385.7 80.1 %all-gather.6.cloned.1.call-start = ((), (), s32[]{:S(2)}) async-start(), calls=%async_computation.2 | async-start | bytes 1081344 | tf_op jit(solution)/shard_map/while/body/eval_jaxpr/all_gather | solution.py:67
  2386.8 3.5 collective-permute-start.1
  2390.3 0.6 copy-start.3
  2465.8 2.5 copy-start
  2468.8 0.6 copy-start.1
  2468.8 0.6 copy-start.2
Sparse Core Ops, SparseCore 0:
  13.5 217.2 reduce-scatter.1
  242.0 212.6 reduce-scatter.1
  465.8 212.6 reduce-scatter.1
  689.7 212.5 reduce-scatter.1
  913.4 212.6 reduce-scatter.1
  1137.3 212.6 reduce-scatter.1
  1361.2 212.6 reduce-scatter.1
  1585.1 212.5 reduce-scatter.1
  1808.5 75.3 all-gather.5
  1892.3 74.7 all-gather.5
  1975.4 74.7 all-gather.5
  2058.5 74.7 all-gather.5
  2141.7 74.7 all-gather.5
  2224.8 74.7 all-gather.5
  2307.9 74.7 all-gather.5
  2391.0 74.7 all-gather.5
where the time goes:
time: 2480 us
  waiting for transfers between devices  2350 us (95%)
  matrix products  63.1 us (3%)
  starting transfers between devices  31.2 us (1%)
    reduce_scatter x8, waiting for transfers between devices, forward_step(): lax.psum_scatter(jnp.einsum('kc,kra->cra', onehot, terms, precision=highe...  1710 us
    all_gather x8, waiting for transfers between devices, backward_step(): lax.all_gather(arrived[None], 'col', axis=0, tiled=True)  600 us
  transfers between devices with their start and end apart: 32, of which 32 were waited for; matrix products, arithmetic and copies ran while one was open for 0% of the time, Pallas kernels for 0%

commit v1 on v0

--- a/solution.py
+++ b/solution.py
@@ -64,7 +64,15 @@
         picked = jnp.einsum(
             "kc,cra->kra",
             onehot,
-            lax.all_gather(arrived[None], "col", axis=0, tiled=True),
+            jnp.concatenate(
+                lax.all_to_all(
+                    jnp.stack([arrived[None]] * lax.psum(1, "col"), 0),
+                    "col",
+                    concat_axis=0,
+                    split_axis=0,
+                ),
+                axis=0,
+            ),
             precision=highest,
         )
         term = jnp.einsum("kra,kab->rb", picked, blocks, precision=highest)

time: 2480 us -> 2150 us (0.87)
  waiting for transfers between devices: 2350 us -> 1970 us
  starting transfers between devices: 31.2 us -> 80.9 us
    all_gather x8 -> x0, waiting for transfers between devices: 600 us -> none  [backward_step(): lax.all_gather(arrived[None], 'col', axis=0, tiled=True)]
    all_to_all x0 -> x8, waiting for transfers between devices: none -> 215 us  [backward_step(): lax.all_to_all(jnp.stack([arrived[None]] * lax.psum(1, 'col'), 0), 'col',...]
    all_to_all x0 -> x8, starting transfers between devices: none -> 49 us  [backward_step(): lax.all_to_all(jnp.stack([arrived[None]] * lax.psum(1, 'col'), 0), 'col',...]
where the time goes in v1:
time: 2150 us
  waiting for transfers between devices  1970 us (92%)
  starting transfers between devices  80.9 us (4%)
  matrix products  53.1 us (2%)
  local copies, waits for them, and re-layouts  22.7 us (1%)
    reduce_scatter x8, waiting for transfers between devices, forward_step(): lax.psum_scatter(jnp.einsum('kc,kra->cra', onehot, terms, precision=highe...  1710 us
    all_to_all x8, waiting for transfers between devices, backward_step(): lax.all_to_all(jnp.stack([arrived[None]] * lax.psum(1, 'col'), 0), 'col',...  215 us
    ppermute x16, waiting for transfers between devices, shifted(): lax.ppermute(value, axis, [(source, source + steps) for source in range(f...  52.2 us
    all_to_all x8, starting transfers between devices, backward_step(): lax.all_to_all(jnp.stack([arrived[None]] * lax.psum(1, 'col'), 0), 'col',...  49 us
  transfers between devices with their start and end apart: 32, of which 32 were waited for; matrix products, arithmetic and copies ran while one was open for 0% of the time, Pallas kernels for 0%

profile of v1, /device:TPU:2, one launch (start us, length us, event | category | flops | bytes accessed | tf_op | source)
XLA Modules:
  0.0 2146.9 jit_solution(5772110562407181234)
XLA Ops:
  7.8 1795.2 %while.35 = (s32[]{:T(128)}, f32[64,128]{1,0:T(8,128)S(1)}, f32[64,128]{1,0:T(8,128)S(1)}, s32[]{:T(128)}, f32[64,128]{1,0:T(8,128)}, /*index=5*/f32[128,128]{1,...) while((s32[]{:T(128)}, f32[64,128]{1,0:T(8,128)S(1)}, ...), condition=%wide.region_2.3_spmd.clone, body=%wide.region_0.2_spmd.clone.sunk | while | flops 138461696 | bytes 7930159 | solution.py:54
  9.0 1.7 fusion.53
  13.4 217.5 %reduce-scatter.2.cloned.1.call-done = f32[1,64,128]{2,1,0:T(8,128)} async-done(((f32[32,64,128]{2,1,0:T(8,128)}), f32[1,64,128]{2,1,0:T(8,128)}) %reduce-scatter.2.cloned.1.call-update) | async-done | bytes 32784 | tf_op jit(solution)/shard_map/while/body/eval_jaxpr/reduce_scatter | solution.py:41
  230.9 1.9 collective-permute-start
  232.8 3.5 collective-permute-done
  237.5 1.7 fusion.53
  241.9 212.8 %reduce-scatter.2.cloned.1.call-done = f32[1,64,128]{2,1,0:T(8,128)} async-done(((f32[32,64,128]{2,1,0:T(8,128)}), f32[1,64,128]{2,1,0:T(8,128)}) %reduce-scatter.2.cloned.1.call-update) | async-done | bytes 32784 | tf_op jit(solution)/shard_map/while/body/eval_jaxpr/reduce_scatter | solution.py:41
  454.6 1.9 collective-permute-start
  456.6 3.5 collective-permute-done
  461.3 1.7 fusion.53
  465.7 212.8 %reduce-scatter.2.cloned.1.call-done = f32[1,64,128]{2,1,0:T(8,128)} async-done(((f32[32,64,128]{2,1,0:T(8,128)}), f32[1,64,128]{2,1,0:T(8,128)}) %reduce-scatter.2.cloned.1.call-update) | async-done | bytes 32784 | tf_op jit(solution)/shard_map/while/body/eval_jaxpr/reduce_scatter | solution.py:41
  678.5 1.9 collective-permute-start
  680.4 3.5 collective-permute-done
  685.1 1.7 fusion.53
  689.5 212.8 %reduce-scatter.2.cloned.1.call-done = f32[1,64,128]{2,1,0:T(8,128)} async-done(((f32[32,64,128]{2,1,0:T(8,128)}), f32[1,64,128]{2,1,0:T(8,128)}) %reduce-scatter.2.cloned.1.call-update) | async-done | bytes 32784 | tf_op jit(solution)/shard_map/while/body/eval_jaxpr/reduce_scatter | solution.py:41
  902.3 1.9 collective-permute-start
  904.2 3.5 collective-permute-done
  908.9 1.7 fusion.53
  913.3 212.7 %reduce-scatter.2.cloned.1.call-done = f32[1,64,128]{2,1,0:T(8,128)} async-done(((f32[32,64,128]{2,1,0:T(8,128)}), f32[1,64,128]{2,1,0:T(8,128)}) %reduce-scatter.2.cloned.1.call-update) | async-done | bytes 32784 | tf_op jit(solution)/shard_map/while/body/eval_jaxpr/reduce_scatter | solution.py:41
  1126.1 1.9 collective-permute-start
  1128.0 3.5 collective-permute-done
  1132.7 1.7 fusion.53
  1137.1 212.8 %reduce-scatter.2.cloned.1.call-done = f32[1,64,128]{2,1,0:T(8,128)} async-done(((f32[32,64,128]{2,1,0:T(8,128)}), f32[1,64,128]{2,1,0:T(8,128)}) %reduce-scatter.2.cloned.1.call-update) | async-done | bytes 32784 | tf_op jit(solution)/shard_map/while/body/eval_jaxpr/reduce_scatter | solution.py:41
  1349.9 1.9 collective-permute-start
  1351.9 3.5 collective-permute-done
  1356.5 1.7 fusion.53
  1361.0 212.8 %reduce-scatter.2.cloned.1.call-done = f32[1,64,128]{2,1,0:T(8,128)} async-done(((f32[32,64,128]{2,1,0:T(8,128)}), f32[1,64,128]{2,1,0:T(8,128)}) %reduce-scatter.2.cloned.1.call-update) | async-done | bytes 32784 | tf_op jit(solution)/shard_map/while/body/eval_jaxpr/reduce_scatter | solution.py:41
  1573.8 1.9 collective-permute-start
  1575.7 3.5 collective-permute-done
  1580.4 1.7 fusion.53
  1584.8 212.7 %reduce-scatter.2.cloned.1.call-done = f32[1,64,128]{2,1,0:T(8,128)} async-done(((f32[32,64,128]{2,1,0:T(8,128)}), f32[1,64,128]{2,1,0:T(8,128)}) %reduce-scatter.2.cloned.1.call-update) | async-done | bytes 32784 | tf_op jit(solution)/shard_map/while/body/eval_jaxpr/reduce_scatter | solution.py:41
  1797.6 1.9 collective-permute-start
  1799.5 3.5 collective-permute-done
  1803.0 336.4 %while.36 = (s32[]{:T(128)}, f32[64,128]{1,0:T(8,128)S(1)}, f32[64,128]{1,0:T(8,128)S(1)}, s32[]{:T(128)}, f32[64,128]{1,0:T(8,128)S(1)}, /*index=5*/f32[128,128...) while((s32[]{:T(128)}, f32[64,128]{1,0:T(8,128)S(1)}, ...), condition=%wide.region_4.5_spmd.clone, body=%wide.region_3.4_spmd.clone.sunk | while | flops 138461696 | bytes 8847691 | solution.py:84
  1804.1 1.9 collective-permute-start.1
  1808.7 6.8 all-to-all-start
  1815.5 28.2 %all-to-all-done = f32[32,1,64,128]{3,2,1,0:T(8,128)S(1)} async-done(((f32[32,1,64,128]{3,2,1,0:T(8,128)}), f32[32,1,64,128]{3,2,1,0:T(8,128)S(1)}, u32[]{:S(2)}, u32[]{:S(2)}) %all-to-all-start) | async-done | bytes 1048608 | tf_op jit(solution)/shard_map/while/body/eval_jaxpr/all_to_all | solution.py:68
  1846.6 2.3 collective-permute-start.1
  1851.6 6.3 all-to-all-start
  1857.9 27.0 %all-to-all-done = f32[32,1,64,128]{3,2,1,0:T(8,128)S(1)} async-done(((f32[32,1,64,128]{3,2,1,0:T(8,128)}), f32[32,1,64,128]{3,2,1,0:T(8,128)S(1)}, u32[]{:S(2)}, u32[]{:S(2)}) %all-to-all-start) | async-done | bytes 1048608 | tf_op jit(solution)/shard_map/while/body/eval_jaxpr/all_to_all | solution.py:68
  1887.7 2.5 collective-permute-start.1
  1890.2 2.8 collective-permute-done.1
  1894.1 6.1 all-to-all-start
  1900.2 26.9 %all-to-all-done = f32[32,1,64,128]{3,2,1,0:T(8,128)S(1)} async-done(((f32[32,1,64,128]{3,2,1,0:T(8,128)}), f32[32,1,64,128]{3,2,1,0:T(8,128)S(1)}, u32[]{:S(2)}, u32[]{:S(2)}) %all-to-all-start) | async-done | bytes 1048608 | tf_op jit(solution)/shard_map/while/body/eval_jaxpr/all_to_all | solution.py:68
  1929.9 1.9 collective-permute-start.1
  1931.8 3.5 collective-permute-done.1
  1936.4 6.0 all-to-all-start
  1942.5 26.8 %all-to-all-done = f32[32,1,64,128]{3,2,1,0:T(8,128)S(1)} async-done(((f32[32,1,64,128]{3,2,1,0:T(8,128)}), f32[32,1,64,128]{3,2,1,0:T(8,128)S(1)}, u32[]{:S(2)}, u32[]{:S(2)}) %all-to-all-start) | async-done | bytes 1048608 | tf_op jit(solution)/shard_map/while/body/eval_jaxpr/all_to_all | solution.py:68
  1972.1 1.9 collective-permute-start.1
  1974.0 3.5 collective-permute-done.1
  1978.7 6.0 all-to-all-start
  1984.7 26.8 %all-to-all-done = f32[32,1,64,128]{3,2,1,0:T(8,128)S(1)} async-done(((f32[32,1,64,128]{3,2,1,0:T(8,128)}), f32[32,1,64,128]{3,2,1,0:T(8,128)S(1)}, u32[]{:S(2)}, u32[]{:S(2)}) %all-to-all-start) | async-done | bytes 1048608 | tf_op jit(solution)/shard_map/while/body/eval_jaxpr/all_to_all | solution.py:68
  2014.3 1.9 collective-permute-start.1
  2016.2 3.6 collective-permute-done.1
  2020.9 6.0 all-to-all-start
  2026.9 26.7 %all-to-all-done = f32[32,1,64,128]{3,2,1,0:T(8,128)S(1)} async-done(((f32[32,1,64,128]{3,2,1,0:T(8,128)}), f32[32,1,64,128]{3,2,1,0:T(8,128)S(1)}, u32[]{:S(2)}, u32[]{:S(2)}) %all-to-all-start) | async-done | bytes 1048608 | tf_op jit(solution)/shard_map/while/body/eval_jaxpr/all_to_all | solution.py:68
  2056.5 1.9 collective-permute-start.1
  2058.4 3.7 collective-permute-done.1
  2063.2 5.9 all-to-all-start
  2069.2 26.6 %all-to-all-done = f32[32,1,64,128]{3,2,1,0:T(8,128)S(1)} async-done(((f32[32,1,64,128]{3,2,1,0:T(8,128)}), f32[32,1,64,128]{3,2,1,0:T(8,128)S(1)}, u32[]{:S(2)}, u32[]{:S(2)}) %all-to-all-start) | async-done | bytes 1048608 | tf_op jit(solution)/shard_map/while/body/eval_jaxpr/all_to_all | solution.py:68
  2098.6 1.9 collective-permute-start.1
  2100.5 3.8 collective-permute-done.1
  2105.4 5.9 all-to-all-start
  2111.3 26.4 %all-to-all-done = f32[32,1,64,128]{3,2,1,0:T(8,128)S(1)} async-done(((f32[32,1,64,128]{3,2,1,0:T(8,128)}), f32[32,1,64,128]{3,2,1,0:T(8,128)S(1)}, u32[]{:S(2)}, u32[]{:S(2)}) %all-to-all-start) | async-done | bytes 1048608 | tf_op jit(solution)/shard_map/while/body/eval_jaxpr/all_to_all | solution.py:68
  (108 shorter events, 65.9 us)
Async XLA Ops:
  7.2 0.7 copy-start.3
  7.8 223.0 %reduce-scatter.2.cloned.1.call-start = ((), (), s32[]{:S(2)}) async-start(), calls=%async_computation.2 | async-start | bytes 1081344 | tf_op jit(solution)/shard_map/while/body/eval_jaxpr/reduce_scatter | solution.py:41
  230.9 5.4 collective-permute-start
  236.3 218.3 %reduce-scatter.2.cloned.1.call-start = ((), (), s32[]{:S(2)}) async-start(), calls=%async_computation.2 | async-start | bytes 1081344 | tf_op jit(solution)/shard_map/while/body/eval_jaxpr/reduce_scatter | solution.py:41
  454.6 5.4 collective-permute-start
  460.1 218.4 %reduce-scatter.2.cloned.1.call-start = ((), (), s32[]{:S(2)}) async-start(), calls=%async_computation.2 | async-start | bytes 1081344 | tf_op jit(solution)/shard_map/while/body/eval_jaxpr/reduce_scatter | solution.py:41
  678.5 5.4 collective-permute-start
  683.9 218.4 %reduce-scatter.2.cloned.1.call-start = ((), (), s32[]{:S(2)}) async-start(), calls=%async_computation.2 | async-start | bytes 1081344 | tf_op jit(solution)/shard_map/while/body/eval_jaxpr/reduce_scatter | solution.py:41
  902.3 5.4 collective-permute-start
  907.7 218.3 %reduce-scatter.2.cloned.1.call-start = ((), (), s32[]{:S(2)}) async-start(), calls=%async_computation.2 | async-start | bytes 1081344 | tf_op jit(solution)/shard_map/while/body/eval_jaxpr/reduce_scatter | solution.py:41
  1126.1 5.4 collective-permute-start
  1131.5 218.4 %reduce-scatter.2.cloned.1.call-start = ((), (), s32[]{:S(2)}) async-start(), calls=%async_computation.2 | async-start | bytes 1081344 | tf_op jit(solution)/shard_map/while/body/eval_jaxpr/reduce_scatter | solution.py:41
  1349.9 5.4 collective-permute-start
  1355.4 218.4 %reduce-scatter.2.cloned.1.call-start = ((), (), s32[]{:S(2)}) async-start(), calls=%async_computation.2 | async-start | bytes 1081344 | tf_op jit(solution)/shard_map/while/body/eval_jaxpr/reduce_scatter | solution.py:41
  1573.8 5.4 collective-permute-start
  1579.2 218.3 %reduce-scatter.2.cloned.1.call-start = ((), (), s32[]{:S(2)}) async-start(), calls=%async_computation.2 | async-start | bytes 1081344 | tf_op jit(solution)/shard_map/while/body/eval_jaxpr/reduce_scatter | solution.py:41
  1797.6 5.4 collective-permute-start
  1804.1 3.5 collective-permute-start.1
  1808.7 35.1 %all-to-all-start = ((f32[32,1,64,128]{3,2,1,0:T(8,128)}), f32[32,1,64,128]{3,2,1,0:T(8,128)S(1)}, u32[]{:S(2)}, u32[]{:S(2)}) async-start(f32[32,1,64,128]{3,2,1,0:T(8,128)} %stack.7), calls=%async_computation.1 | async-start | bytes 2097152 | tf_op jit(solution)/shard_map/while/body/eval_jaxpr/all_to_all | solution.py:68
  1843.8 1.3 copy-start
  1846.6 4.0 collective-permute-start.1
  1851.6 33.3 %all-to-all-start = ((f32[32,1,64,128]{3,2,1,0:T(8,128)}), f32[32,1,64,128]{3,2,1,0:T(8,128)S(1)}, u32[]{:S(2)}, u32[]{:S(2)}) async-start(f32[32,1,64,128]{3,2,1,0:T(8,128)} %stack.7), calls=%async_computation.1 | async-start | bytes 2097152 | tf_op jit(solution)/shard_map/while/body/eval_jaxpr/all_to_all | solution.py:68
  1884.9 1.3 copy-start
  1887.7 5.3 collective-permute-start.1
  1894.1 33.0 %all-to-all-start = ((f32[32,1,64,128]{3,2,1,0:T(8,128)}), f32[32,1,64,128]{3,2,1,0:T(8,128)S(1)}, u32[]{:S(2)}, u32[]{:S(2)}) async-start(f32[32,1,64,128]{3,2,1,0:T(8,128)} %stack.7), calls=%async_computation.1 | async-start | bytes 2097152 | tf_op jit(solution)/shard_map/while/body/eval_jaxpr/all_to_all | solution.py:68
  1927.1 1.3 copy-start
  1929.9 5.4 collective-permute-start.1
  1936.4 32.9 %all-to-all-start = ((f32[32,1,64,128]{3,2,1,0:T(8,128)}), f32[32,1,64,128]{3,2,1,0:T(8,128)S(1)}, u32[]{:S(2)}, u32[]{:S(2)}) async-start(f32[32,1,64,128]{3,2,1,0:T(8,128)} %stack.7), calls=%async_computation.1 | async-start | bytes 2097152 | tf_op jit(solution)/shard_map/while/body/eval_jaxpr/all_to_all | solution.py:68
  1969.3 1.3 copy-start
  1972.1 5.5 collective-permute-start.1
  1978.7 32.8 %all-to-all-start = ((f32[32,1,64,128]{3,2,1,0:T(8,128)}), f32[32,1,64,128]{3,2,1,0:T(8,128)S(1)}, u32[]{:S(2)}, u32[]{:S(2)}) async-start(f32[32,1,64,128]{3,2,1,0:T(8,128)} %stack.7), calls=%async_computation.1 | async-start | bytes 2097152 | tf_op jit(solution)/shard_map/while/body/eval_jaxpr/all_to_all | solution.py:68
  2011.5 1.3 copy-start
  2014.3 5.5 collective-permute-start.1
  2020.9 32.7 %all-to-all-start = ((f32[32,1,64,128]{3,2,1,0:T(8,128)}), f32[32,1,64,128]{3,2,1,0:T(8,128)S(1)}, u32[]{:S(2)}, u32[]{:S(2)}) async-start(f32[32,1,64,128]{3,2,1,0:T(8,128)} %stack.7), calls=%async_computation.1 | async-start | bytes 2097152 | tf_op jit(solution)/shard_map/while/body/eval_jaxpr/all_to_all | solution.py:68
  2053.7 1.3 copy-start
  2056.5 5.6 collective-permute-start.1
  2063.2 32.6 %all-to-all-start = ((f32[32,1,64,128]{3,2,1,0:T(8,128)}), f32[32,1,64,128]{3,2,1,0:T(8,128)S(1)}, u32[]{:S(2)}, u32[]{:S(2)}) async-start(f32[32,1,64,128]{3,2,1,0:T(8,128)} %stack.7), calls=%async_computation.1 | async-start | bytes 2097152 | tf_op jit(solution)/shard_map/while/body/eval_jaxpr/all_to_all | solution.py:68
  2095.8 1.3 copy-start
  2098.6 5.8 collective-permute-start.1
  2105.4 32.3 %all-to-all-start = ((f32[32,1,64,128]{3,2,1,0:T(8,128)}), f32[32,1,64,128]{3,2,1,0:T(8,128)S(1)}, u32[]{:S(2)}, u32[]{:S(2)}) async-start(f32[32,1,64,128]{3,2,1,0:T(8,128)} %stack.7), calls=%async_computation.1 | async-start | bytes 2097152 | tf_op jit(solution)/shard_map/while/body/eval_jaxpr/all_to_all | solution.py:68
  2137.7 1.3 copy-start
  2139.5 0.6 copy-start.1
  2139.5 0.6 copy-start.2
Sparse Core Ops, SparseCore 0:
  13.5 217.3 reduce-scatter.1
  242.0 212.5 reduce-scatter.1
  465.8 212.6 reduce-scatter.1
  689.6 212.6 reduce-scatter.1
  913.5 212.5 reduce-scatter.1
  1137.2 212.6 reduce-scatter.1
  1361.1 212.6 reduce-scatter.1
  1584.9 212.5 reduce-scatter.1
